TPU v7x, 128 devices: a whole 4x4x4 slice. The times are simulated.
128 devices in a mesh: grp: 2 (over core), row: 16 (over y, x), col: 4 (over z).
Axes of the slice: x: 4, y: 4, z: 4, core: 2. Of those that a mesh axis runs over, the one named last changes fastest.
Arguments:
- root_inverse: bfloat16 [12288, 12288], P(('grp', 'row'), 'col'), may hold values from -0.0546875 to 0.0546875
- child_inverse: bfloat16 [2, 8192, 8192], P('grp', 'row', 'col'), may hold values from -0.0625 to 0.0625
- coupling: bfloat16 [2, 1536, 8192], P('grp', 'col', 'row'), may hold values from -0.0625 to 0.0625
- child_weights: bfloat16 [2, 8192], P('grp', 'col'), may hold values from 0.5 to 2
- root_weights: bfloat16 [12288], P('col'), may hold values from 0.5 to 2
- parent_blocks: int32 [2, 12], replicated, may hold values from 0 to 95, as said below
Outputs:
- grad_root: bfloat16 [12288, 12288], P(('grp', 'row'), 'col')
- grad_child: bfloat16 [2, 8192, 8192], P('grp', 'row', 'col')
- grad_coupling: bfloat16 [2, 1536, 8192], P('grp', 'col', 'row')
Inputs may be any that keep to these rules, and one draw needn't show every extreme that they name: `parent_blocks`: within one child the 12 blocks are distinct; child 0 always names block 0 and block 12288 // 128 - 1; the two children may share blocks.
All inputs are finite; a program needn't handle non-finite values.
Results may differ from a plain program's by a relative error of at most 0.0059.
Values may be sent and summed in bfloat16 or wider, within the bound.
A program may use at most 128 MiB of HBM per device.

v0:
```python
import jax
import jax.numpy as jnp
from jax import lax
from jax.sharding import PartitionSpec as P

BW = 128


def local(root_inverse, child_inverse, coupling, child_weights, root_weights, parent_blocks):
    col_index = lax.axis_index("col")
    col_count = lax.axis_size("col")
    root_rows, root_cols = root_inverse.shape
    local_blocks = root_cols // BW
    share_cols = coupling.shape[1]
    width = share_cols * col_count
    block_count = width // BW
    highest = lax.Precision.HIGHEST
    offset = parent_blocks - col_index * local_blocks
    block_ids = jnp.arange(local_blocks, dtype=jnp.int32)
    owners = [
        (offset[child][:, None] == block_ids[None, :]).astype(jnp.float32) for child in range(2)
    ]
    root_blocks = root_inverse.astype(jnp.float32).reshape(root_rows, local_blocks, BW)
    picks = []
    for child in range(2):
        taken = jnp.einsum("rkb,jk->rjb", root_blocks, owners[child], precision=highest)
        picks.append(taken.reshape(root_rows, width))
    picked = jnp.stack(picks, axis=1)
    selected = lax.psum(picked.astype(jnp.bfloat16), "col")
    mine = lax.dynamic_slice_in_dim(selected, col_index * share_cols, share_cols, 2)
    margin_part = jnp.concatenate(
        [
            jnp.dot(selected[:, child, :].T, mine[:, child, :], preferred_element_type=jnp.float32)
            for child in range(2)
        ],
        axis=0,
    )
    margin = lax.psum_scatter(margin_part, ("grp", "row"), scatter_dimension=0, tiled=True).astype(
        jnp.bfloat16
    )
    factor = child_inverse[0]
    links = coupling[0]
    weights = child_weights[0].astype(jnp.float32)
    links_all = lax.all_gather(links, "col", axis=0, tiled=True)
    solved = lax.psum_scatter(
        jnp.dot(links_all, factor, preferred_element_type=jnp.float32),
        "row",
        scatter_dimension=0,
        tiled=True,
    ).astype(jnp.bfloat16)
    solved_all = lax.all_gather(solved, "row", axis=0, tiled=True)
    scaled = (solved.astype(jnp.float32) * weights[None, :]).astype(jnp.bfloat16)
    adjoint_t = lax.psum_scatter(
        jnp.dot(solved_all, scaled.T, preferred_element_type=jnp.float32),
        "col",
        scatter_dimension=0,
        tiled=True,
    ).astype(jnp.bfloat16)
    adjoint_cols = lax.all_gather(adjoint_t, ("grp", "row"), axis=1, tiled=True).reshape(
        share_cols, 2, width
    )
    lifted = jnp.stack(
        [
            jnp.dot(
                selected[:, child, :],
                adjoint_cols[:, child, :].T,
                preferred_element_type=jnp.float32,
            )
            for child in range(2)
        ],
        axis=1,
    ).astype(jnp.bfloat16)
    lifted_all = lax.all_gather(lifted, "col", axis=2, tiled=True).reshape(
        root_rows, 2, block_count, BW
    )
    placed = jnp.zeros((root_rows, local_blocks, BW), jnp.float32)
    for child in range(2):
        spread = lifted_all[:, child].astype(jnp.float32)
        placed = placed + jnp.einsum("rjb,jk->rkb", spread, owners[child], precision=highest)
    placed = placed.reshape(root_rows, root_cols)
    root_scale = root_weights.astype(jnp.float32)[None, :]
    grad_root = (2.0 * root_inverse.astype(jnp.float32) * root_scale + 2.0 * placed).astype(
        jnp.bfloat16
    )
    margin_row = lax.all_gather(margin, "col", axis=1, tiled=True)
    pulled = (
        2.0 * jnp.dot(margin_row, solved_all, preferred_element_type=jnp.float32) * weights[None, :]
    ).astype(jnp.bfloat16)
    pulled_all = lax.all_gather(pulled, "row", axis=0, tiled=True)
    grad_links = lax.psum_scatter(
        jnp.dot(pulled_all, factor.T, preferred_element_type=jnp.float32),
        "col",
        scatter_dimension=0,
        tiled=True,
    ).astype(jnp.bfloat16)
    grad_factor = jnp.dot(links_all.T, pulled_all, preferred_element_type=jnp.float32)
    grad_factor = (grad_factor + 2.0 * factor.astype(jnp.float32) * weights[None, :]).astype(
        jnp.bfloat16
    )
    return (grad_root, grad_factor[None], grad_links[None])


def solution(mesh):
    return jax.shard_map(
        local,
        mesh=mesh,
        in_specs=(
            P(("grp", "row"), "col"),
            P("grp", "row", "col"),
            P("grp", "col", "row"),
            P("grp", "col"),
            P("col"),
            P(),
        ),
        out_specs=(P(("grp", "row"), "col"), P("grp", "row", "col"), P("grp", "col", "row")),
        check_vma=False,
    )
```

profile of v0, /device:TPU:1, one launch (start us, length us, event | category | flops | bytes accessed | tf_op | source)
XLA Modules:
  0.0 578.5 jit_solution(17137444513439801942)
XLA Ops:
  7.9 31.4 %all-gather.15.cloned.1.call-done = bf16[1,1536,512]{2,1,0:T(8,128)(2,1)} async-done(((bf16[1,384,512]{2,1,0:T(8,128)(2,1)}), bf16[1,1536,512]{2,1,0:T(8,128)(2,1)}) %all-gather.15.cloned.1.call-update) | async-done | bytes 1572880 | tf_op jit(solution)/shard_map/all_gather | solution.py:44
  39.4 10.0 %fusion.6 = f32[1536,2048]{1,0:T(8,128)} fusion(bf16[1,512,2048]{2,1,0:T(8,128)(2,1)} %param.7, bf16[1,1536,512]{2,1,0:T(8,128)(2,1)} %all-gather.15.cloned.1.call-done), kind=kOutput, calls=%fused_computation.12 | convolution fusion | flops 3221225472 | bytes 16252928 | tf_op jit(solution)/shard_map/dot_general | solution.py:46
  49.5 94.5 %reduce-scatter.5.cloned.1.call-done = f32[96,2048]{1,0:T(8,128)} async-done(((f32[1536,2048]{1,0:T(8,128)}), f32[96,2048]{1,0:T(8,128)}) %reduce-scatter.5.cloned.1.call-update) | async-done | bytes 786448 | tf_op jit(solution)/shard_map/reduce_scatter | solution.py:45
  146.0 2.2 copy.20
  159.1 48.1 %all-gather.7.cloned.1.call-done = bf16[1536,2048]{1,0:T(8,128)(2,1)} async-done(((bf16[96,2048]{1,0:T(8,128)(2,1)}), bf16[1536,2048]{1,0:T(8,128)(2,1)}) %all-gather.7.cloned.1.call-update) | async-done | bytes 6291472 | tf_op jit(solution)/shard_map/all_gather | solution.py:51
  207.2 5.7 fusion.19
  213.0 60.0 %all-reduce.2.cloned.1.call-done = bf16[384,2,1536]{0,2,1:T(8,128)(2,1)} async-done(((bf16[384,2,1536]{0,2,1:T(8,128)(2,1)}), bf16[384,2,1536]{0,2,1:T(8,128)(2,1)}) %all-reduce.2.cloned.1.call-update) | async-done | bytes 2359312 | tf_op jit(solution)/shard_map/psum | solution.py:29
  273.0 2.4 fusion.17
  276.3 2.5 pad_maximum_fusion
  278.9 16.9 %reduce-scatter.7.cloned.1.call-done = f32[384,96]{0,1:T(8,128)} async-done(((f32[1536,96]{0,1:T(8,128)}), f32[384,96]{0,1:T(8,128)}) %reduce-scatter.7.cloned.1.call-update) | async-done | bytes 147472 | tf_op jit(solution)/shard_map/reduce_scatter | solution.py:53
  297.5 85.5 %reduce-scatter.9.cloned.1.call-done = f32[96,384]{1,0:T(8,128)} async-done(((f32[3072,384]{1,0:T(8,128)}), f32[96,384]{1,0:T(8,128)}) %reduce-scatter.9.cloned.1.call-update) | async-done | bytes 147472 | tf_op jit(solution)/shard_map/reduce_scatter | solution.py:38
  383.9 10.0 %all_gather.22 = bf16[96,1536]{1,0:T(8,128)(2,1)S(1)} all-gather(bf16[96,384]{1,0:T(8,128)(2,1)S(1)} %convert_element_type.52), channel_id=1, replica_groups=mesh['grp'=2,'row'=16,'col'=4] {'col'}, dimensions={1}, use_global_device_ids=true | all-gather | bytes 368640 | tf_op jit(solution)/shard_map/all_gather | solution.py:85
  394.0 4.7 fusion.3
  399.0 32.1 %all-gather.9.cloned.1.call-done = bf16[384,3072]{0,1:T(8,128)(2,1)} async-done(((bf16[384,96]{0,1:T(8,128)(2,1)}), bf16[384,3072]{0,1:T(8,128)(2,1)}) %all-gather.9.cloned.1.call-update) | async-done | bytes 2359312 | tf_op jit(solution)/shard_map/all_gather | solution.py:59
  435.0 58.7 %all-gather.13.cloned.1.call-done = bf16[1536,2048]{1,0:T(8,128)(2,1)} async-done(((bf16[96,2048]{1,0:T(8,128)(2,1)}), bf16[1536,2048]{1,0:T(8,128)(2,1)}) %all-gather.13.cloned.1.call-update) | async-done | bytes 6291472 | tf_op jit(solution)/shard_map/all_gather | solution.py:89
  493.8 8.6 %fusion.4 = f32[1536,512]{1,0:T(8,128)} fusion(bf16[1536,2048]{1,0:T(8,128)(2,1)} %all-gather.13.cloned.1.call-done, bf16[1,512,2048]{2,1,0:T(8,128)(2,1)} %param.7), kind=kOutput, calls=%fused_computation.10 | convolution fusion | flops 3221225472 | bytes 11534336 | tf_op jit(solution)/shard_map/dot_general | solution.py:91
  504.0 2.5 copy.13
  506.5 22.5 %all-gather.11.cloned.1.call-done = bf16[384,2,1536]{2,0,1:T(8,128)(2,1)} async-done(((bf16[384,2,384]{2,0,1:T(8,128)(2,1)}), bf16[384,2,1536]{2,0,1:T(8,128)(2,1)}) %all-gather.11.cloned.1.call-update) | async-done | bytes 2359312 | tf_op jit(solution)/shard_map/all_gather | solution.py:73
  528.9 3.0 copy.14
  534.7 2.3 copy.19
  540.0 2.9 fusion
  542.9 3.7 fusion.2
  546.6 2.4 copy.17
  549.0 20.8 %reduce-scatter.11.cloned.1.call-done = f32[384,512]{1,0:T(8,128)} async-done(((f32[1536,512]{1,0:T(8,128)}), f32[384,512]{1,0:T(8,128)}) %reduce-scatter.11.cloned.1.call-update) | async-done | bytes 786448 | tf_op jit(solution)/shard_map/reduce_scatter | solution.py:90
  (75 shorter events, 30.5 us)
Async XLA Ops:
  7.2 32.2 %all-gather.15.cloned.1.call-start = ((), (), s32[]{:S(2)}) async-start(), calls=%async_computation.13 | async-start | bytes 1966080 | tf_op jit(solution)/shard_map/all_gather | solution.py:44
  7.9 136.1 %reduce-scatter.5.cloned.1.call-start = ((), (), s32[]{:S(2)}) async-start(), calls=%async_computation.5 | async-start | bytes 13369344 | tf_op jit(solution)/shard_map/reduce_scatter | solution.py:45
  49.4 157.8 %all-gather.7.cloned.1.call-start = ((), (), s32[]{:S(2)}) async-start(), calls=%async_computation.6 | async-start | bytes 6684672 | tf_op jit(solution)/shard_map/all_gather | solution.py:51
  145.9 127.1 %all-reduce.2.cloned.1.call-start = ((), (), s32[]{:S(2)}) async-start(), calls=%async_computation.4 | async-start | bytes 4718592 | tf_op jit(solution)/shard_map/psum | solution.py:29
  146.0 2.3 copy-start.11
  158.4 48.8 %copy-start.1 = (bf16[96,2048]{1,0:T(8,128)(2,1)S(1)}, bf16[96,2048]{1,0:T(8,128)(2,1)}, u32[]{:S(2)}) copy-start(bf16[96,2048]{1,0:T(8,128)(2,1)} %convert_element_type.47) | copy-start | bytes 1179652
  158.4 137.4 %reduce-scatter.7.cloned.1.call-start = ((), (), s32[]{:S(2)}) async-start(), calls=%async_computation.7 | async-start | bytes 737280 | tf_op jit(solution)/shard_map/reduce_scatter | solution.py:53
  212.9 170.1 %reduce-scatter.9.cloned.1.call-start = ((), (), s32[]{:S(2)}) async-start(), calls=%async_computation.10 | async-start | bytes 4866048 | tf_op jit(solution)/shard_map/reduce_scatter | solution.py:38
  273.0 2.4 copy-start.2
  278.8 152.2 %all-gather.9.cloned.1.call-start = ((), (), s32[]{:S(2)}) async-start(), calls=%async_computation.8 | async-start | bytes 2433024 | tf_op jit(solution)/shard_map/all_gather | solution.py:59
  297.4 196.4 %all-gather.13.cloned.1.call-start = ((), (), s32[]{:S(2)}) async-start(), calls=%async_computation.11 | async-start | bytes 6684672 | tf_op jit(solution)/shard_map/all_gather | solution.py:89
  297.5 101.2 %copy-start.5 = (f32[2048]{0:T(1024)}, f32[2048]{0:T(1024)S(1)}, u32[]{:S(2)}) copy-start(f32[2048]{0:T(1024)S(1)} %broadcast_multiply_fusion) | copy-start | bytes 24580
  398.7 130.2 %all-gather.11.cloned.1.call-start = ((), (), s32[]{:S(2)}) async-start(), calls=%async_computation.9 | async-start | bytes 2949120 | tf_op jit(solution)/shard_map/all_gather | solution.py:73
  431.0 2.2 copy-start.12
  435.0 134.8 %reduce-scatter.11.cloned.1.call-start = ((), (), s32[]{:S(2)}) async-start(), calls=%async_computation.12 | async-start | bytes 3932160 | tf_op jit(solution)/shard_map/reduce_scatter | solution.py:90
  502.4 1.6 copy-start.3
  504.0 2.5 copy-start.8
  534.7 2.3 copy-start.10
  537.0 5.8 %slice-start = ((s8[6291456]{0:T(1024)(128)(4,1)}), s8[4194304]{0:T(1024)(128)(4,1)S(1)}, s32[]{:S(2)}) async-start(s8[6291456]{0:T(1024)(128)(4,1)} %bitcast.102), calls=%async_computation.14 | async-start | bytes 8388608
  537.9 2.0 copy-start
  537.9 4.9 slice-start.1
  539.9 2.9 copy-start.4
  539.9 2.9 copy-start.6
  540.0 2.9 copy-start.13
  (2 other events, 1.3 us)
Sparse Core Ops, SparseCore 0:
  9.6 29.7 all-gather.14
  49.5 94.3 reduce-scatter.4
  146.7 60.5 all-gather.6
  210.0 62.8 all-reduce.1
  275.8 19.9 reduce-scatter.6
  299.4 83.5 reduce-scatter.8
  385.8 45.1 all-gather.8
  433.7 59.9 all-gather.12
  496.0 32.8 all-gather.10
  531.2 38.4 reduce-scatter.10
where the time goes:
time: 579 us
  waiting for transfers between devices  471 us (81%)
  matrix products  44.4 us (8%)
  local copies, waits for them, and re-layouts  23.3 us (4%)
  between operations  14.4 us (2%)
  other arithmetic  14.3 us (2%)
  blocking collectives  10 us (2%)
    reduce_scatter x1, waiting for transfers between devices, local(): lax.psum_scatter(jnp.dot(links_all, factor, preferred_element_type=jnp.fl...  94.5 us
    reduce_scatter x1, waiting for transfers between devices, local(): lax.psum_scatter(margin_part, ('grp', 'row'), scatter_dimension=0, tiled=...  85.5 us
    psum x1, waiting for transfers between devices, local(): selected = lax.psum(picked.astype(jnp.bfloat16), 'col')  60 us
    all_gather x1, waiting for transfers between devices, local(): pulled_all = lax.all_gather(pulled, 'row', axis=0, tiled=True)  58.7 us
    all_gather x1, waiting for transfers between devices, local(): solved_all = lax.all_gather(solved, 'row', axis=0, tiled=True)  48.1 us
    all_gather x1, waiting for transfers between devices, local(): lax.all_gather(adjoint_t, ('grp', 'row'), axis=1, tiled=True)  32.1 us
    all_gather x1, waiting for transfers between devices, local(): links_all = lax.all_gather(links, 'col', axis=0, tiled=True)  31.4 us
    all_gather x1, waiting for transfers between devices, local(): lax.all_gather(lifted, 'col', axis=2, tiled=True)  22.5 us
  transfers between devices with their start and end apart: 10, of which 10 were waited for; matrix products, arithmetic and copies ran while one was open for 11% of the time, Pallas kernels for 0%

commit v1 on v0

--- a/solution.py
+++ b/solution.py
@@ -26,7 +26,12 @@
         taken = jnp.einsum("rkb,jk->rjb", root_blocks, owners[child], precision=highest)
         picks.append(taken.reshape(root_rows, width))
     picked = jnp.stack(picks, axis=1)
-    selected = lax.psum(picked.astype(jnp.bfloat16), "col")
+
+    def launch_sources_all_for(x0):
+        passed = jnp.sum(lax.all_gather(x0, axis_name="col"), 0)
+        return passed
+
+    selected = launch_sources_all_for(picked.astype(jnp.bfloat16))
     mine = lax.dynamic_slice_in_dim(selected, col_index * share_cols, share_cols, 2)
     margin_part = jnp.concatenate(
         [

time: 579 us -> 609 us (1.052)
  waiting for transfers between devices: 471 us -> 493 us
    all_gather x0 -> x1, waiting for transfers between devices: none -> 87.9 us  [launch_sources_all_for(): passed = jnp.sum(lax.all_gather(x0, axis_name='col'), 0)]
    psum x1 -> x0, waiting for transfers between devices: 60 us -> none  [local(): selected = lax.psum(picked.astype(jnp.bfloat16), 'col')]
    unnamed x37 -> x35, local copies, waits for them, and re-layouts: 14.7 us -> 14.7 us
  transfers between devices with their start and end apart: 10 -> 10, of which waited for: 10 -> 10; matrix products, arithmetic and copies ran while one was open for 11% -> 12% of each run, Pallas kernels for 0% -> 0%
where the time goes in v1:
time: 609 us; the launch traced here: 608 us
  waiting for transfers between devices  493 us (81%)
  matrix products  42.9 us (7%)
  local copies, waits for them, and re-layouts  26.5 us (4%)
  other arithmetic  20 us (3%)
  between operations  14.4 us (2%)
  blocking collectives  10 us (2%)
    reduce_scatter x1, waiting for transfers between devices, local(): lax.psum_scatter(jnp.dot(links_all, factor, preferred_element_type=jnp.fl...  94.5 us
    all_gather x1, waiting for transfers between devices, launch_sources_all_for(): passed = jnp.sum(lax.all_gather(x0, axis_name='col'), 0)  87.9 us
    reduce_scatter x1, waiting for transfers between devices, local(): lax.psum_scatter(margin_part, ('grp', 'row'), scatter_dimension=0, tiled=...  85.6 us
    all_gather x1, waiting for transfers between devices, local(): pulled_all = lax.all_gather(pulled, 'row', axis=0, tiled=True)  58.6 us
    all_gather x1, waiting for transfers between devices, local(): solved_all = lax.all_gather(solved, 'row', axis=0, tiled=True)  45.1 us
    all_gather x1, waiting for transfers between devices, local(): lax.all_gather(adjoint_t, ('grp', 'row'), axis=1, tiled=True)  32.2 us
    all_gather x1, waiting for transfers between devices, local(): links_all = lax.all_gather(links, 'col', axis=0, tiled=True)  31.4 us
    all_gather x1, waiting for transfers between devices, local(): lax.all_gather(lifted, 'col', axis=2, tiled=True)  22.5 us
  transfers between devices with their start and end apart: 10, of which 10 were waited for; matrix products, arithmetic and copies ran while one was open for 12% of the time, Pallas kernels for 0%

profile of v1, /device:TPU:1, one launch (start us, length us, event | category | flops | bytes accessed | tf_op | source)
XLA Modules:
  0.0 607.9 jit_solution(6036884127559897906)
XLA Ops:
  7.9 31.4 %all-gather.18.cloned.1.call-done = bf16[1,1536,512]{2,1,0:T(8,128)(2,1)} async-done(((bf16[1,384,512]{2,1,0:T(8,128)(2,1)}), bf16[1,1536,512]{2,1,0:T(8,128)(2,1)}) %all-gather.18.cloned.1.call-update) | async-done | bytes 1572880 | tf_op jit(solution)/shard_map/all_gather | solution.py:49
  39.4 10.0 %fusion.6 = f32[1536,2048]{1,0:T(8,128)} fusion(bf16[1,512,2048]{2,1,0:T(8,128)(2,1)} %param.7, bf16[1,1536,512]{2,1,0:T(8,128)(2,1)} %all-gather.18.cloned.1.call-done), kind=kOutput, calls=%fused_computation.12 | convolution fusion | flops 3221225472 | bytes 16252928 | tf_op jit(solution)/shard_map/dot_general | solution.py:51
  49.5 94.5 %reduce-scatter.5.cloned.1.call-done = f32[96,2048]{1,0:T(8,128)} async-done(((f32[1536,2048]{1,0:T(8,128)}), f32[96,2048]{1,0:T(8,128)}) %reduce-scatter.5.cloned.1.call-update) | async-done | bytes 786448 | tf_op jit(solution)/shard_map/reduce_scatter | solution.py:50
  154.6 2.7 copy.19
  158.9 2.6 copy.20
  162.2 45.1 %all-gather.10.cloned.1.call-done = bf16[1536,2048]{1,0:T(8,128)(2,1)} async-done(((bf16[96,2048]{1,0:T(8,128)(2,1)}), bf16[1536,2048]{1,0:T(8,128)(2,1)}) %all-gather.10.cloned.1.call-update) | async-done | bytes 6291472 | tf_op jit(solution)/shard_map/all_gather | solution.py:56
  207.2 5.7 fusion.19
  213.2 87.9 %all-gather.8.cloned.1.call-done = bf16[4,384,2,1536]{3,1,2,0:T(8,128)(2,1)} async-done(((bf16[1,384,2,1536]{3,1,2,0:T(8,128)(2,1)}), bf16[4,384,2,1536]{3,1,2,0:T(8,128)(2,1)}) %all-gather.8.cloned.1.call-update) | async-done | bytes 9437200 | tf_op jit(solution)/shard_map/all_gather | solution.py:31
  301.1 5.9 reduce_sum.12
  308.9 2.4 pad_maximum_fusion
  311.4 13.8 %reduce-scatter.7.cloned.1.call-done = f32[384,96]{0,1:T(8,128)} async-done(((f32[1536,96]{0,1:T(8,128)}), f32[384,96]{0,1:T(8,128)}) %reduce-scatter.7.cloned.1.call-update) | async-done | bytes 147472 | tf_op jit(solution)/shard_map/reduce_scatter | solution.py:58
  326.9 85.6 %reduce-scatter.9.cloned.1.call-done = f32[96,384]{1,0:T(8,128)} async-done(((f32[3072,384]{1,0:T(8,128)}), f32[96,384]{1,0:T(8,128)}) %reduce-scatter.9.cloned.1.call-update) | async-done | bytes 147472 | tf_op jit(solution)/shard_map/reduce_scatter | solution.py:43
  413.3 10.0 %all_gather.27 = bf16[96,1536]{1,0:T(8,128)(2,1)S(1)} all-gather(bf16[96,384]{1,0:T(8,128)(2,1)S(1)} %convert_element_type.61), channel_id=1, replica_groups=mesh['grp'=2,'row'=16,'col'=4] {'col'}, dimensions={1}, use_global_device_ids=true | all-gather | bytes 368640 | tf_op jit(solution)/shard_map/all_gather | solution.py:90
  423.4 4.7 fusion.3
  428.2 32.2 %all-gather.12.cloned.1.call-done = bf16[384,3072]{0,1:T(8,128)(2,1)} async-done(((bf16[384,96]{0,1:T(8,128)(2,1)}), bf16[384,3072]{0,1:T(8,128)(2,1)}) %all-gather.12.cloned.1.call-update) | async-done | bytes 2359312 | tf_op jit(solution)/shard_map/all_gather | solution.py:64
  464.6 58.6 %all-gather.16.cloned.1.call-done = bf16[1536,2048]{1,0:T(8,128)(2,1)} async-done(((bf16[96,2048]{1,0:T(8,128)(2,1)}), bf16[1536,2048]{1,0:T(8,128)(2,1)}) %all-gather.16.cloned.1.call-update) | async-done | bytes 6291472 | tf_op jit(solution)/shard_map/all_gather | solution.py:94
  523.2 8.6 %fusion.4 = f32[1536,512]{1,0:T(8,128)} fusion(bf16[1536,2048]{1,0:T(8,128)(2,1)} %all-gather.16.cloned.1.call-done, bf16[1,512,2048]{2,1,0:T(8,128)(2,1)} %param.7), kind=kOutput, calls=%fused_computation.10 | convolution fusion | flops 3221225472 | bytes 11534336 | tf_op jit(solution)/shard_map/dot_general | solution.py:96
  533.4 2.5 copy.23
  535.9 22.5 %all-gather.14.cloned.1.call-done = bf16[384,2,1536]{2,0,1:T(8,128)(2,1)} async-done(((bf16[384,2,384]{2,0,1:T(8,128)(2,1)}), bf16[384,2,1536]{2,0,1:T(8,128)(2,1)}) %all-gather.14.cloned.1.call-update) | async-done | bytes 2359312 | tf_op jit(solution)/shard_map/all_gather | solution.py:78
  558.3 3.0 copy.25
  569.4 2.9 fusion
  572.3 3.7 fusion.2
  576.0 2.4 copy.30
  578.4 20.8 %reduce-scatter.11.cloned.1.call-done = f32[384,512]{1,0:T(8,128)} async-done(((f32[1536,512]{1,0:T(8,128)}), f32[384,512]{1,0:T(8,128)}) %reduce-scatter.11.cloned.1.call-update) | async-done | bytes 786448 | tf_op jit(solution)/shard_map/reduce_scatter | solution.py:95
  (75 shorter events, 33.9 us)
Async XLA Ops:
  7.2 32.2 %all-gather.18.cloned.1.call-start = ((), (), s32[]{:S(2)}) async-start(), calls=%async_computation.13 | async-start | bytes 1966080 | tf_op jit(solution)/shard_map/all_gather | solution.py:49
  7.9 136.1 %reduce-scatter.5.cloned.1.call-start = ((), (), s32[]{:S(2)}) async-start(), calls=%async_computation.5 | async-start | bytes 13369344 | tf_op jit(solution)/shard_map/reduce_scatter | solution.py:50
  49.4 157.8 %all-gather.10.cloned.1.call-start = ((), (), s32[]{:S(2)}) async-start(), calls=%async_computation.6 | async-start | bytes 6684672 | tf_op jit(solution)/shard_map/all_gather | solution.py:56
  145.9 155.2 %all-gather.8.cloned.1.call-start = ((), (), s32[]{:S(2)}) async-start(), calls=%async_computation.4 | async-start | bytes 11796480 | tf_op jit(solution)/shard_map/all_gather | solution.py:31
  146.0 2.3 copy-start.10
  161.5 0.7 copy-start.6
  161.5 45.8 %copy-start.1 = (bf16[96,2048]{1,0:T(8,128)(2,1)S(1)}, bf16[96,2048]{1,0:T(8,128)(2,1)}, u32[]{:S(2)}) copy-start(bf16[96,2048]{1,0:T(8,128)(2,1)} %convert_element_type.56) | copy-start | bytes 1179652
  161.5 163.7 %reduce-scatter.7.cloned.1.call-start = ((), (), s32[]{:S(2)}) async-start(), calls=%async_computation.7 | async-start | bytes 737280 | tf_op jit(solution)/shard_map/reduce_scatter | solution.py:58
  212.9 199.5 %reduce-scatter.9.cloned.1.call-start = ((), (), s32[]{:S(2)}) async-start(), calls=%async_computation.10 | async-start | bytes 4866048 | tf_op jit(solution)/shard_map/reduce_scatter | solution.py:43
  311.4 149.0 %all-gather.12.cloned.1.call-start = ((), (), s32[]{:S(2)}) async-start(), calls=%async_computation.8 | async-start | bytes 2433024 | tf_op jit(solution)/shard_map/all_gather | solution.py:64
  326.8 196.4 %all-gather.16.cloned.1.call-start = ((), (), s32[]{:S(2)}) async-start(), calls=%async_computation.11 | async-start | bytes 6684672 | tf_op jit(solution)/shard_map/all_gather | solution.py:94
  326.8 101.3 %copy-start.4 = (f32[2048]{0:T(1024)}, f32[2048]{0:T(1024)S(1)}, u32[]{:S(2)}) copy-start(f32[2048]{0:T(1024)S(1)} %broadcast_multiply_fusion) | copy-start | bytes 24580
  428.1 130.2 %all-gather.14.cloned.1.call-start = ((), (), s32[]{:S(2)}) async-start(), calls=%async_computation.9 | async-start | bytes 2949120 | tf_op jit(solution)/shard_map/all_gather | solution.py:78
  460.4 2.2 copy-start.11
  464.3 134.8 %reduce-scatter.11.cloned.1.call-start = ((), (), s32[]{:S(2)}) async-start(), calls=%async_computation.12 | async-start | bytes 3932160 | tf_op jit(solution)/shard_map/reduce_scatter | solution.py:95
  531.8 1.6 copy-start.2
  533.4 2.5 copy-start.7
  564.1 2.3 copy-start.9
  566.4 5.8 slice-start
  567.3 2.0 copy-start
  567.3 4.9 slice-start.1
  569.3 2.9 copy-start.3
  569.3 2.9 copy-start.5
  569.3 2.9 copy-start.12
  (1 other events, 0.6 us)
Sparse Core Ops, SparseCore 0:
  9.6 29.7 all-gather.17
  49.5 94.3 reduce-scatter.4
  146.7 60.5 all-gather.9
  209.3 91.7 all-gather.7
  303.9 21.2 reduce-scatter.6
  328.8 83.5 reduce-scatter.8
  415.2 45.1 all-gather.11
  463.1 59.9 all-gather.15
  525.4 32.8 all-gather.13
  560.6 38.4 reduce-scatter.10
